TPU v7x, 32 devices: a whole 2x2x4 slice. The times are simulated.
32 devices in a mesh: group: 4 (over x, core), head: 8 (over z, y).
Axes of the slice: x: 2, y: 2, z: 4, core: 2. Of those that a mesh axis runs over, the one named last changes fastest.
Arguments:
- qkv: bfloat16 [2048, 3, 512], P(('group', 'head')), may hold values from -40 to 40
- pattern: int32 [4, 3, 8, 6], P('group'), may hold values from 0 to 7, as said below
- counts: int32 [4, 3, 8], P('group'), may hold values from 0 to 6, as said below
Outputs:
- attended: bfloat16 [2048, 512], P(('group', 'head'))
Inputs may be any that keep to these rules, and one draw needn't show every extreme that they name: `pattern`: within one list (g, j, n) the 6 blocks are distinct; at offset index 1 the first entry of query block n's list is n. `counts`: at offset index 1 every count is 1 or more; some count equals 6.
All inputs are finite; a program needn't handle non-finite values.
Results may differ from a plain program's by a relative error of at most 0.0044.
Values may be sent and summed in bfloat16 or wider, within the bound.
No kernel may reach another device: no remote copies, remote signals or barrier semaphores. Data moves between devices by JAX's collectives and lax.ppermute only.
A program may use at most 64 MiB of HBM per device.

v0:
```python
import jax
import jax.numpy as jnp
from jax import lax
from jax.sharding import PartitionSpec as P

BLOCK = 64


def from_behind(value, axis, steps):
    count = lax.axis_size(axis)
    pairs = [(source, (source + steps) % count) for source in range(count)]
    return lax.ppermute(value, axis, pairs)


def body(qkv, pattern, counts):
    half = lax.axis_size("group") // 4
    gathered = lax.all_to_all(qkv, "head", split_axis=2, concat_axis=0, tiled=True)
    group_rows = gathered.shape[0]
    head_dim = gathered.shape[2]
    blocks = group_rows // BLOCK
    query = gathered[:, 0].reshape(blocks, BLOCK, head_dim)
    paired = jnp.concatenate([gathered[:, 1], gathered[:, 2]], axis=-1)
    lists = pattern[0]
    live_counts = counts[0]
    scale = head_dim ** (-0.5)

    def attend(state, source, offset, keep):
        chosen = lax.dynamic_index_in_dim(lists, offset, 0, keepdims=False)
        number = lax.dynamic_index_in_dim(live_counts, offset, 0, keepdims=False) * keep
        width = chosen.shape[1]
        tiles = source.reshape(blocks, BLOCK, 2 * head_dim)[chosen]
        tiles = tiles.reshape(blocks, width * BLOCK, 2 * head_dim)
        key_part = tiles[..., :head_dim]
        value_part = tiles[..., head_dim:]
        scores = (
            jnp.einsum("nqd,nkd->nqk", query, key_part, preferred_element_type=jnp.float32) * scale
        )
        live = (jnp.arange(width * BLOCK, dtype=jnp.int32) // BLOCK)[None, :] < number[:, None]
        scores = jnp.where(live[:, None, :], scores, -jnp.inf)
        running, total, accum = state
        newmax = jnp.maximum(running, scores.max(axis=-1))
        weights = jnp.exp(scores - newmax[..., None])
        factor = jnp.exp(running - newmax)
        total = total * factor + weights.sum(axis=-1)
        accum = accum * factor[..., None] + jnp.einsum(
            "nqk,nkd->nqd",
            weights.astype(jnp.bfloat16),
            value_part,
            preferred_element_type=jnp.float32,
        )
        return (newmax, total, accum)

    start = (
        jnp.full((blocks, BLOCK), -jnp.inf, jnp.float32),
        jnp.zeros((blocks, BLOCK), jnp.float32),
        jnp.zeros((blocks, BLOCK, head_dim), jnp.float32),
    )
    state = attend(start, paired, half, jnp.int32(1))

    def both_step(step_index, carry):
        ahead, behind, state = carry
        ahead = from_behind(ahead, "group", 1)
        behind = from_behind(behind, "group", -1)
        state = attend(state, ahead, half - step_index, jnp.int32(1))
        state = attend(state, behind, half + step_index, jnp.int32(1))
        return (ahead, behind, state)

    ahead, behind, state = lax.fori_loop(1, half + 1, both_step, (paired, paired, state))
    running, total, accum = state
    output = (accum / total[..., None]).astype(jnp.bfloat16).reshape(group_rows, head_dim)
    return lax.all_to_all(output, "head", split_axis=0, concat_axis=1, tiled=True)


def solution(mesh):
    return jax.shard_map(
        body,
        mesh=mesh,
        in_specs=(
            P(("group", "head"), None, None),
            P("group", None, None, None),
            P("group", None, None),
        ),
        out_specs=P(("group", "head"), None),
        check_vma=False,
    )
```

profile of v0, /device:TPU:0, one launch (start us, length us, event | category | flops | bytes accessed | tf_op | source)
XLA Modules:
  0.0 40.3 jit_solution(15031859175372729375)
XLA Ops:
  0.0 1.2 %copy.19 = bf16[64,3,512]{0,1,2:T(4,128)(2,1)S(1)} copy(bf16[64,3,512]{2,0,1:T(8,128)(2,1)} %param.3) | data formatting | bytes 393216 | tf_op args[0]
  1.2 1.0 %reshape.303 = bf16[8,2,6144]{2,1,0:T(2,128)(2,1)} reshape(bf16[512,3,64]{2,1,0:T(4,128)(2,1)S(1)} %bitcast.55) | data formatting | bytes 393216
  2.3 7.4 %all-to-all-start = ((bf16[8,2,6144]{2,1,0:T(2,128)(2,1)}), bf16[8,2,6144]{2,1,0:T(2,128)(2,1)S(1)}, u32[]{:S(2)}, u32[]{:S(2)}) async-start(bf16[8,2,6144]{2,1,0:T(2,128)(2,1)} %reshape.303), calls=%async_computation | async-start | bytes 393216 | tf_op jit(solution)/shard_map/all_to_all | solution.py:17
  9.8 0.1 copy.24
  9.8 0.1 reshape.283
  9.9 0.1 copy.21
  10.0 0.1 reshape.275
  10.1 0.1 copy.27
  10.2 0.1 reshape.291
  10.4 7.3 %all-to-all-done = bf16[8,2,6144]{2,1,0:T(2,128)(2,1)S(1)} async-done(((bf16[8,2,6144]{2,1,0:T(2,128)(2,1)}), bf16[8,2,6144]{2,1,0:T(2,128)(2,1)S(1)}, u32[]{:S(2)}, u32[]{:S(2)}) %all-to-all-start) | async-done | bytes 196640 | tf_op jit(solution)/shard_map/all_to_all | solution.py:17
  17.7 0.3 reshape.304
  18.0 0.3 copy.20
  18.4 0.1 pad_maximum_fusion.1
  18.6 0.5 %collective-permute-start = (bf16[512,128]{1,0:T(8,128)(2,1)S(1)}, bf16[512,128]{1,0:T(8,128)(2,1)S(1)}, u32[]{:S(2)}, u32[]{:S(2)}) collective-permute-start(bf16[512,128]{1,0:T(8,128)(2,1)S(1)} %pad_maximum_fusion.1), channel_id=1, source_target_pairs={{0,8},{8,16},{16,24},{24,0},{1,9},{9,17},{17,25},{25,1},{2,10},{10... | collective-permute-start | bytes 393224 | tf_op jit(solution)/shard_map/while/body/eval_jaxpr/ppermute | solution.py:12
  19.1 0.1 pad_maximum_fusion
  19.2 0.7 %gather_fusion = bf16[48,64,128]{2,1,0:T(8,128)(2,1)S(1)} fusion(bf16[8,64,128]{2,1,0:T(8,128)(2,1)S(1)} %pad_maximum_fusion, s32[1024]{0:T(1024)S(1)} %pad_clamp_fusion.2), kind=kCustom, calls=%fused_computation | custom fusion | bytes 1573056 | tf_op jit(solution)/shard_map/gather | solution.py:31
  19.9 0.5 %fusion.32 = (f32[8,64]{1,0:T(8,128)S(1)}, f32[8,64,384]{2,1,0:T(8,128)S(1)}) fusion(bf16[8,64,64]{2,1,0:T(8,128)(2,1)S(1)} %bitcast.56, bf16[8,384,128]{2,1,0:T(8,128)(2,1)S(1)} %bitcast.46, pred[8,384]{1,0:T(8,128)(4,1)S(1)} %get-tuple-element.51), kind=kOutput, calls=%fused_computation.65 | convolution fusion | flops 25755136 | bytes 1643520 | tf_op jit(solution)/shard_map/nqd,nkd->nqk/dot_general | solution.py:36
  20.4 0.3 fusion.16
  20.8 3.7 %collective-permute-done = bf16[512,128]{1,0:T(8,128)(2,1)S(1)} collective-permute-done((bf16[512,128]{1,0:T(8,128)(2,1)S(1)}, bf16[512,128]{1,0:T(8,128)(2,1)S(1)}, u32[]{:S(2)}, u32[]{:S(2)}) %collective-permute-start) | collective-permute-done | bytes 131104 | tf_op jit(solution)/shard_map/while/body/eval_jaxpr/ppermute | solution.py:12
  24.4 0.7 %gather_fusion.1 = bf16[48,64,128]{2,1,0:T(8,128)(2,1)S(1)} fusion(bf16[8,64,128]{2,1,0:T(8,128)(2,1)S(1)} %bitcast.51, s32[1024]{0:T(1024)S(1)} %pad_clamp_fusion.1), kind=kCustom, calls=%fused_computation.1 | custom fusion | bytes 1573056 | tf_op jit(solution)/shard_map/while/body/eval_jaxpr/gather | solution.py:31
  25.1 0.7 %gather_fusion.2 = bf16[48,64,128]{2,1,0:T(8,128)(2,1)S(1)} fusion(bf16[8,64,128]{2,1,0:T(8,128)(2,1)S(1)} %bitcast.50, s32[1024]{0:T(1024)S(1)} %pad_clamp_fusion), kind=kCustom, calls=%fused_computation.2 | custom fusion | bytes 1573056 | tf_op jit(solution)/shard_map/while/body/eval_jaxpr/gather | solution.py:31
  25.8 0.5 %fusion.33 = (f32[8,64]{1,0:T(8,128)S(1)}, f32[8,64,384]{2,1,0:T(8,128)S(1)}) fusion(bf16[8,64,64]{2,1,0:T(8,128)(2,1)S(1)} %bitcast.57, bf16[8,384,128]{2,1,0:T(8,128)(2,1)S(1)} %bitcast.52, pred[8,384]{1,0:T(8,128)(4,1)S(1)} %get-tuple-element.50), kind=kOutput, calls=%fused_computation.66 | convolution fusion | flops 25755136 | bytes 1643520 | tf_op jit(solution)/shard_map/while/body/eval_jaxpr/nqd,nkd->nqk/dot_general | solution.py:36
  26.4 0.5 %fusion.34 = (f32[8,64]{1,0:T(8,128)S(1)}, f32[8,64,384]{2,1,0:T(8,128)S(1)}) fusion(bf16[8,64,64]{2,1,0:T(8,128)(2,1)S(1)} %bitcast.58, bf16[8,384,128]{2,1,0:T(8,128)(2,1)S(1)} %bitcast.48, pred[8,384]{1,0:T(8,128)(4,1)S(1)} %get-tuple-element.49), kind=kOutput, calls=%fused_computation.67 | convolution fusion | flops 25755136 | bytes 1643520 | tf_op jit(solution)/shard_map/while/body/eval_jaxpr/nqd,nkd->nqk/dot_general | solution.py:36
  26.9 0.5 %fusion.18 = (f32[8,64]{1,0:T(8,128)S(1)}, f32[8,64]{1,0:T(8,128)S(1)}) fusion(f32[8,64,384]{2,1,0:T(8,128)S(1)} %get-tuple-element.60, f32[8,64]{1,0:T(8,128)S(1)} %get-tuple-element.27, f32[8,64,384]{2,1,0:T(8,128)S(1)} %get-tuple-element.58, f32[8,64]{1,0:T(8,128)S(1)} %get-tuple-element.26), kind=kLoop, calls=%fused_computation.30 | loop fusion | flops 785408 | bytes 1581056 | tf_op jit(solution)/shard_map/while/body/eval_jaxpr/reduce_sum | solution.py:44
  27.5 0.6 %fusion.8 = f32[8,64,64]{2,1,0:T(8,128)S(1)} fusion(bf16[8,384,128]{2,1,0:T(8,128)(2,1)S(1)} %bitcast.47, f32[8,64,384]{2,1,0:T(8,128)S(1)} %get-tuple-element.56, f32[8,64]{1,0:T(8,128)S(1)} %get-tuple-element.55, f32[8,64]{1,0:T(8,128)S(1)} %get-tuple-element.25, f32[8,64]{1,0:T(8,128)S(1)} %get-tuple-element.48), kind=kOutput, calls=%fused_computation.17 | convolution fusion | flops 25624576 | bytes 1710080 | tf_op jit(solution)/shard_map/nqk,nkd->nqd/dot_general | solution.py:45
  28.1 0.6 %fusion.7 = f32[8,64,64]{2,1,0:T(8,128)S(1)} fusion(f32[8,64,64]{2,1,0:T(8,128)S(1)} %fusion.8, bf16[8,384,128]{2,1,0:T(8,128)(2,1)S(1)} %bitcast.49, f32[8,64,384]{2,1,0:T(8,128)S(1)} %get-tuple-element.60, f32[8,64]{1,0:T(8,128)S(1)} %get-tuple-element.27, f32[8,64]{1,0:T(8,128)S(1)} %get-tuple-element.24), kind=kOutput, calls=%fused_computation.15 | convolution fusion | flops 25624576 | bytes 1839104 | tf_op jit(solution)/shard_map/while/body/eval_jaxpr/nqk,nkd->nqd/dot_general | solution.py:45
  28.7 0.6 %fusion.9 = bf16[8,64,64]{2,1,0:T(8,128)(2,1)S(1)} fusion(f32[8,64,64]{2,1,0:T(8,128)S(1)} %fusion.7, bf16[8,384,128]{2,1,0:T(8,128)(2,1)S(1)} %bitcast.53, f32[8,64,384]{2,1,0:T(8,128)S(1)} %get-tuple-element.58, f32[8,64]{1,0:T(8,128)S(1)} %get-tuple-element.26, f32[8,64]{1,0:T(8,128)S(1)} %get-tuple-element.23), kind=kOutput, calls=%fused_computation.18 | convolution fusion | flops 25657344 | bytes 1773568 | tf_op jit(solution)/shard_map/while/body/eval_jaxpr/nqk,nkd->nqd/dot_general | solution.py:45
  29.2 0.2 reshape.305
  29.4 9.8 %all_to_all.34 = bf16[8,2,2048]{2,1,0:T(2,128)(2,1)S(1)} all-to-all(bf16[8,2,2048]{2,1,0:T(2,128)(2,1)S(1)} %reshape.305), channel_id=1, replica_groups=mesh['group'=4,'head'=8] {'head'}, dimensions={0} | all-to-all | bytes 131072 | tf_op jit(solution)/shard_map/all_to_all | solution.py:71
  39.2 0.1 reshape.306
  39.4 0.1 copy.30
  39.5 0.8 %all_to_all.31 = bf16[64,512]{1,0:T(8,128)(2,1)} reshape(bf16[64,8,64]{2,1,0:T(8,128)(2,1)S(1)} %copy.30) | data formatting | bytes 131072 | tf_op jit(solution)/shard_map/all_to_all | solution.py:71
  (16 shorter events, 0.3 us)
Async XLA Ops:
  2.3 7.4 %copy-start.1 = (s32[1,3,8]{2,0,1:T(1,128)S(1)}, s32[1,3,8]{2,0,1:T(1,128)}, u32[]{:S(2)}) copy-start(s32[1,3,8]{2,0,1:T(1,128)} %param.5) | copy-start | bytes 292
  2.3 7.5 %copy-start = (s32[1,3,8,6]{2,0,3,1:T(1,128)S(1)}, s32[1,3,8,6]{2,0,3,1:T(1,128)}, u32[]{:S(2)}) copy-start(s32[1,3,8,6]{2,0,3,1:T(1,128)} %param.4) | copy-start | bytes 1732
  2.3 15.4 %all-to-all-start = ((bf16[8,2,6144]{2,1,0:T(2,128)(2,1)}), bf16[8,2,6144]{2,1,0:T(2,128)(2,1)S(1)}, u32[]{:S(2)}, u32[]{:S(2)}) async-start(bf16[8,2,6144]{2,1,0:T(2,128)(2,1)} %reshape.303), calls=%async_computation | async-start | bytes 393216 | tf_op jit(solution)/shard_map/all_to_all | solution.py:17
  18.5 6.6 %collective-permute-start.1 = (bf16[512,128]{1,0:T(8,128)(2,1)S(1)}, bf16[512,128]{1,0:T(8,128)(2,1)S(1)}, u32[]{:S(2)}, u32[]{:S(2)}) collective-permute-start(bf16[512,128]{1,0:T(8,128)(2,1)S(1)} %pad_maximum_fusion.1), channel_id=1, source_target_pairs={{0,24},{8,0},{16,8},{24,16},{1,25},{9,1},{17,9},{25,17},{2,26},{10... | collective-permute-start | bytes 393224 | tf_op jit(solution)/shard_map/while/body/eval_jaxpr/ppermute | solution.py:12
  18.6 5.8 %collective-permute-start = (bf16[512,128]{1,0:T(8,128)(2,1)S(1)}, bf16[512,128]{1,0:T(8,128)(2,1)S(1)}, u32[]{:S(2)}, u32[]{:S(2)}) collective-permute-start(bf16[512,128]{1,0:T(8,128)(2,1)S(1)} %pad_maximum_fusion.1), channel_id=1, source_target_pairs={{0,8},{8,16},{16,24},{24,0},{1,9},{9,17},{17,25},{25,1},{2,10},{10... | collective-permute-start | bytes 393224 | tf_op jit(solution)/shard_map/while/body/eval_jaxpr/ppermute | solution.py:12
where the time goes:
time: 40.6 us; the launch traced here: 40.3 us
  waiting for transfers between devices  11 us (27%)
  blocking collectives  9.85 us (24%)
  starting transfers between devices  7.99 us (20%)
  local copies, waits for them, and re-layouts  6.72 us (17%)
  matrix products  3.38 us (8%)
  other arithmetic  1.19 us (3%)
    all_to_all x1, blocking collectives, body(): lax.all_to_all(output, 'head', split_axis=0, concat_axis=1, tiled=True)  9.85 us
    all_to_all x1, starting transfers between devices, body(): lax.all_to_all(qkv, 'head', split_axis=2, concat_axis=0, tiled=True)  7.44 us
    all_to_all x1, waiting for transfers between devices, body(): lax.all_to_all(qkv, 'head', split_axis=2, concat_axis=0, tiled=True)  7.3 us
    ppermute x2, waiting for transfers between devices, from_behind(): return lax.ppermute(value, axis, pairs)  3.65 us
    unnamed x9, local copies, waits for them, and re-layouts  2.87 us
    gather x3, local copies, waits for them, and re-layouts, attend(): tiles = source.reshape(blocks, BLOCK, 2 * head_dim)[chosen]  2.09 us
    dot_general x3, matrix products, attend(): jnp.einsum('nqk,nkd->nqd', weights.astype(jnp.bfloat16), value_part, pref...  1.75 us
    dot_general x3, matrix products, attend(): jnp.einsum('nqd,nkd->nqk', query, key_part, preferred_element_type=jnp.fl...  1.63 us
  transfers between devices with their start and end apart: 3, of which 2 were waited for; matrix products, arithmetic and copies ran while one was open for 7% of the time, Pallas kernels for 0%

commit v1 on v0

v1 whole, which is shorter than its diff:
```python
import functools
import math

import jax
import jax.numpy as jnp
from jax import lax
from jax.experimental import pallas as pl
from jax.experimental.pallas import tpu as pltpu
from jax.sharding import PartitionSpec as P

LOG2E = 1.4426950408889634
VMEM = pltpu.MemorySpace.VMEM
SMEM = pltpu.MemorySpace.SMEM


def lanes_of(shape):
    return lax.broadcasted_iota(jnp.int32, shape, len(shape) - 1)


def rows_dot(left, right):
    return lax.dot_general(
        left, right, (((1,), (1,)), ((), ())), preferred_element_type=jnp.float32
    )


def pack_kernel(dim, x_ref, o_ref):
    tokens = x_ref.shape[1]
    half = tokens // 2
    for head in range(o_ref.shape[0]):
        cols = slice(head * dim, (head + 1) * dim)
        o_ref[head, :tokens] = jnp.concatenate([x_ref[1, :, cols], x_ref[2, :, cols]], axis=-1)
        o_ref[head, tokens:] = jnp.concatenate(
            [x_ref[0, :half, cols], x_ref[0, half:, cols]], axis=-1
        )


def unpack_kernel(dim, x_ref, o_ref):
    half = x_ref.shape[1]
    for pair in range(x_ref.shape[0] // 2):
        one, two = x_ref[2 * pair], x_ref[2 * pair + 1]
        cols = slice(pair * 2 * dim, (pair + 1) * 2 * dim)
        o_ref[:half, cols] = jnp.concatenate([one[:, :dim], two[:, :dim]], axis=-1)
        o_ref[half:, cols] = jnp.concatenate([one[:, dim:], two[:, dim:]], axis=-1)


def padded_queries(packed, dim):
    wide = packed.astype(jnp.float32)
    low = lanes_of(wide.shape) < dim
    top = jnp.where(low, wide, 0.0)
    bottom = jnp.where(low, pltpu.roll(wide, dim, 1), 0.0)
    return jnp.concatenate([top, bottom], axis=0).astype(jnp.bfloat16)


def offset_of(kind, half):
    if kind not in ("near", "far"):
        return kind
    side = 1 - 2 * (lax.axis_index("group") % 2)
    return half + side if kind == "near" else half - side


def dense_bias(lists_ref, counts_ref, offset, block, tile):
    blocks, width = lists_ref.shape[3], lists_ref.shape[1]
    lane = lanes_of((blocks, tile))
    ident = lax.broadcasted_iota(jnp.int32, (blocks, tile), 0)
    found = []
    for first in range(0, blocks, tile // block):
        listed = jnp.zeros((blocks, tile), jnp.int32)
        for n in range(first, first + tile // block):
            here = lane // block == n - first
            number = counts_ref[offset, 0, n]
            for e in range(width):
                entry = jnp.where(e < number, lists_ref[offset, e, 0, n], -1)
                listed = jnp.where(here & (ident == entry), 1, listed)
        found.append(jnp.where(listed > 0, 0.0, -jnp.inf))
    return found


def attend_kernel(dim, dense, kinds, half, first, last, tile, bias_for, *refs):
    refs = list(refs)
    chunk_ref = refs.pop(0)
    sources = [refs.pop(0) for _ in kinds[first:]]
    lists_ref, counts_ref = refs.pop(0), refs.pop(0)
    state_ref = None if first else refs.pop(0)
    out_ref = refs.pop(0)
    query_ref = refs.pop(0) if first else chunk_ref
    blocks = chunk_ref.shape[0]
    block = sources[0].shape[1]
    per = tile // block
    factor = LOG2E / math.sqrt(dim)
    offsets = [offset_of(kind, half) for kind in kinds]
    if first:
        sources = [chunk_ref] + sources
        for n in range(blocks):
            query_ref[n] = padded_queries(chunk_ref[n, block:], dim)

    def values_of(keys):
        return jnp.transpose(keys)[dim:]

    if dense:
        biases = []
        for part, offset in enumerate(offsets):
            if first:
                biases.append(dense_bias(lists_ref, counts_ref, offset, block, tile))
            else:
                biases.append([state_ref[t, dim + 16 :] for t in range(blocks // per)])
        keys = [ref[:, :block].reshape(blocks * block, 2 * dim) for ref in sources]
        values = [values_of(k) for k in keys]
        following = dense_bias(lists_ref, counts_ref, offset_of(bias_for, half), block, tile) if bias_for else None

    def listed(part, n):
        ref, width = sources[part], lists_ref.shape[1]
        at = offsets[part]
        found = jnp.concatenate([ref[lists_ref[at, e, 0, n], :block] for e in range(width)], axis=0)
        place = lax.broadcasted_iota(jnp.int32, (width * block, 1), 0)
        return found, jnp.where(place < counts_ref[at, 0, n] * block, 0.0, -jnp.inf)

    def one_tile(t):
        scores, picked = [], []
        if dense:
            query = query_ref[t * per : (t + 1) * per].reshape(tile, 2 * dim)
            for part in range(len(sources)):
                score = rows_dot(keys[part], query).reshape(blocks, block, tile)
                score = score + biases[part][t][:, None, :]
                scores.append(score.reshape(blocks * block, tile))
        else:
            for part in range(len(sources)):
                both = [listed(part, t * per + i) for i in range(per)]
                picked.append([values_of(k) for k, _ in both])
                scores.append(jnp.concatenate(
                    [rows_dot(k, query_ref[t * per + i]) + bias for i, (k, bias) in enumerate(both)],
                    axis=1,
                ))
        top = functools.reduce(jnp.maximum, [s.max(axis=0, keepdims=True) for s in scores])
        if not first:
            before = state_ref[t, dim : dim + 1]
            top = jnp.maximum(top, before)
        weights = [jnp.exp2((s - top) * factor) for s in scores]
        total = functools.reduce(jnp.add, [w.sum(axis=0, keepdims=True) for w in weights])
        sums = []
        for part, weight in enumerate(weights):
            rounded = weight.astype(jnp.bfloat16)
            if dense:
                sums.append(jnp.dot(values[part], rounded, preferred_element_type=jnp.float32))
            else:
                sums.append(jnp.concatenate([
                    jnp.dot(v, rounded[:, i * block : (i + 1) * block], preferred_element_type=jnp.float32)
                    for i, v in enumerate(picked[part])
                ], axis=1))
        accum = functools.reduce(jnp.add, sums)
        if not first:
            shrink = jnp.exp2((before - top) * factor)
            total = total + state_ref[t, dim + 8 : dim + 9] * shrink
            accum = accum + state_ref[t, :dim] * shrink
        if not last:
            out_ref[t, :dim] = accum
            out_ref[t, dim : dim + 8] = jnp.broadcast_to(top, (8, tile))
            out_ref[t, dim + 8 : dim + 16] = jnp.broadcast_to(total, (8, tile))
            if dense and following is not None:
                out_ref[t, dim + 16 :] = following[t]
            return
        output = accum * (1.0 / total)
        for i in range(0, per, 2):
            pair = output[:, i * block : (i + 2) * block]
            turned = jnp.concatenate([pair, pltpu.roll(pair, 2 * block - block // 2, 1)], axis=0).T
            out_ref[t * per + i] = turned[: block // 2].astype(out_ref.dtype)
            out_ref[t * per + i + 1] = turned[block : block + block // 2].astype(out_ref.dtype)

    if dense:
        for t in range(blocks // per):
            one_tile(t)
    else:
        pl.loop(0, blocks // per)(one_tile)


TILE_BLOCKS = 2


def attend(chunk, kinds, sources, lists, counts, state, last, dense, dim, half, bias_for=None):
    first = state is None
    block = sources[0].shape[1]
    blocks, width = lists.shape[3], lists.shape[1]
    tile = (TILE_BLOCKS if dense else 2) * block
    if last:
        out = jax.ShapeDtypeStruct((blocks, block // 2, 2 * dim), jnp.bfloat16)
    else:
        rows = dim + 16 + (blocks if dense else 0)
        out = jax.ShapeDtypeStruct((blocks * block // tile, rows, tile), jnp.float32)
    outs = (out, jax.ShapeDtypeStruct((blocks, block, 2 * dim), jnp.bfloat16)) if first else (out,)
    vmem = pl.BlockSpec(memory_space=VMEM)
    smem = pl.BlockSpec(memory_space=SMEM)
    args = [chunk, *sources, lists, counts]
    specs = [vmem] * (1 + len(sources)) + [smem, smem]
    if not first:
        args.append(state)
        specs.append(vmem)
    pairs = len(kinds) * blocks * block * (blocks if dense else width) * block
    result = pl.pallas_call(
        functools.partial(attend_kernel, dim, dense, kinds, half, first, last, tile, bias_for),
        out_shape=outs,
        in_specs=specs,
        out_specs=tuple(vmem for _ in outs),
        cost_estimate=pl.CostEstimate(flops=8 * pairs * dim, bytes_accessed=4 * chunk.size, transcendentals=pairs),
        compiler_params=pltpu.CompilerParams(vmem_limit_bytes=VMEM_LIMIT),
        name="attend_last" if last else "attend",
    )(*args)
    return result if first else result[0]


VMEM_LIMIT = 16 << 20


def body(qkv, pattern, counts):
    n_group, n_head = lax.axis_size("group"), lax.axis_size("head")
    half = n_group // 4
    tokens, _, inner = qkv.shape
    dim = inner // n_head
    lists = jnp.transpose(pattern, (1, 3, 0, 2))
    live = jnp.transpose(counts, (1, 0, 2))
    blocks, width = lists.shape[3], lists.shape[1]
    dense = blocks <= 2 * width
    odd = lax.axis_index("group") % 2
    vmem = pl.BlockSpec(memory_space=VMEM)

    packed = pl.pallas_call(
        functools.partial(pack_kernel, dim),
        out_shape=jax.ShapeDtypeStruct((n_head, tokens * 3 // 2, 2 * dim), qkv.dtype),
        compiler_params=pltpu.CompilerParams(vmem_limit_bytes=VMEM_LIMIT),
        name="pack",
    )(jnp.transpose(qkv, (1, 0, 2)))
    chunk = lax.all_to_all(packed, "head", split_axis=0, concat_axis=0, tiled=True)
    own = chunk[:, :tokens]

    def swap(value, shift):
        pairs = []
        for even in range(shift, n_group + shift, 2):
            one, two = even % n_group, (even + 1) % n_group
            pairs += [(one, two), (two, one)]
        return lax.ppermute(value, "group", pairs)

    far = swap(own, 1)
    near = swap(own, 0)
    settings = dict(dense=dense, dim=dim, half=half)
    state, queries = attend(chunk, (half, "near"), [near], lists, live, None, last=False, bias_for="far", **settings)
    state = attend(queries, ("far",), [far], lists, live, state, last=half == 1, **settings)
    ahead = jnp.where(odd == 1, near, far)
    behind = jnp.where(odd == 1, far, near)
    for step in range(2, half + 1):
        ring = [(source, (source + 1) % n_group) for source in range(n_group)]
        ahead = lax.ppermute(ahead, "group", ring)
        behind = lax.ppermute(behind, "group", [(b, a) for a, b in ring])
        for source, offset in ((ahead, half - step), (behind, half + step)):
            last = step == half and offset > half
            state = attend(queries, (offset,), [source], lists, live, state, last=last, **settings)
    returned = lax.all_to_all(state, "head", split_axis=0, concat_axis=0, tiled=True)
    return pl.pallas_call(
        functools.partial(unpack_kernel, dim),
        out_shape=jax.ShapeDtypeStruct((tokens, inner), qkv.dtype),
        in_specs=[vmem],
        compiler_params=pltpu.CompilerParams(vmem_limit_bytes=VMEM_LIMIT),
        name="unpack",
    )(returned)


def solution(mesh):
    return jax.shard_map(
        body,
        mesh=mesh,
        in_specs=(
            P(("group", "head"), None, None),
            P("group", None, None, None),
            P("group", None, None),
        ),
        out_specs=P(("group", "head"), None),
        check_vma=False,
    )
```

time: 40.6 us -> 34.1 us (0.84)
  blocking collectives: 9.85 us -> 24.9 us
  waiting for transfers between devices: 11 us -> 1.37 us
  starting transfers between devices: 7.99 us -> 1.66 us
  local copies, waits for them, and re-layouts: 6.72 us -> 0.95 us
  Pallas kernels: 0 us -> 4.99 us
  matrix products: 3.38 us -> 0 us
  other arithmetic: 1.19 us -> 0 us
    all_to_all x1 -> x2, blocking collectives: 9.85 us -> 24.9 us  [the longest x1 15.1 us: body(): lax.all_to_all(packed, 'head', split_axis=0, concat_axis=0, tiled=True)]
    all_to_all x1 -> x0, starting transfers between devices: 7.44 us -> none  [body(): lax.all_to_all(qkv, 'head', split_axis=2, concat_axis=0, tiled=True)]
    all_to_all x1 -> x0, waiting for transfers between devices: 7.3 us -> none  [body(): lax.all_to_all(qkv, 'head', split_axis=2, concat_axis=0, tiled=True)]
    pallas_call x0 -> x4, Pallas kernels: none -> 4.99 us  [the longest x2 4.16 us: attend(): pl.pallas_call(functools.partial(attend_kernel, dim, dense, kinds, half,...]
    dot_general x6 -> x0, matrix products: 3.38 us -> none  [the longest x3 1.75 us: attend(): jnp.einsum('nqk,nkd->nqd', weights.astype(jnp.bfloat16), value_part, pref...]
    ppermute x2, waiting for transfers between devices: 3.65 us -> 1.37 us  [swap(): return lax.ppermute(value, 'group', pairs)]
    gather x3 -> x0, local copies, waits for them, and re-layouts: 2.09 us -> none  [attend(): tiles = source.reshape(blocks, BLOCK, 2 * head_dim)[chosen]]
    unnamed x9 -> x6, local copies, waits for them, and re-layouts: 2.87 us -> 0.94 us
  transfers between devices with their start and end apart: 3 -> 2, of which waited for: 2 -> 1; matrix products, arithmetic and copies ran while one was open for 7% -> 0% of each run, Pallas kernels for 0% -> 7%
where the time goes in v1:
time: 34.1 us; the launch traced here: 33.9 us
  blocking collectives  24.9 us (73%)
  Pallas kernels  4.99 us (15%)
  starting transfers between devices  1.66 us (5%)
  waiting for transfers between devices  1.37 us (4%)
  local copies, waits for them, and re-layouts  0.95 us (3%)
    all_to_all x1, blocking collectives, body(): lax.all_to_all(packed, 'head', split_axis=0, concat_axis=0, tiled=True)  15.1 us
    all_to_all x1, blocking collectives, body(): lax.all_to_all(state, 'head', split_axis=0, concat_axis=0, tiled=True)  9.85 us
    pallas_call x2, Pallas kernels, attend(): pl.pallas_call(functools.partial(attend_kernel, dim, dense, kinds, half,...  4.16 us
    ppermute x2, starting transfers between devices, swap(): return lax.ppermute(value, 'group', pairs)  1.66 us
    ppermute x2, waiting for transfers between devices, swap(): return lax.ppermute(value, 'group', pairs)  1.37 us
    unnamed x6, local copies, waits for them, and re-layouts  0.94 us
    pallas_call x1, Pallas kernels, body(): pl.pallas_call(functools.partial(unpack_kernel, dim), out_shape=jax.Shape...  0.71 us
  transfers between devices with their start and end apart: 2, of which 1 were waited for; matrix products, arithmetic and copies ran while one was open for 0% of the time, Pallas kernels for 7%

profile of v1, /device:TPU:0, one launch (start us, length us, event | category | flops | bytes accessed | tf_op | source)
XLA Modules:
  0.0 33.9 jit_solution(13185281464386712615)
XLA Ops:
  0.0 0.0 copy-start
  0.0 0.9 %copy-done = bf16[64,3,512]{2,0,1:T(8,128)(2,1)S(1)} copy-done((bf16[64,3,512]{2,0,1:T(8,128)(2,1)S(1)}, bf16[64,3,512]{2,0,1:T(8,128)(2,1)}, u32[]{:S(2)}) %copy-start) | copy-done | bytes 196632
  0.9 0.1 pack.1
  1.1 15.1 %all_to_all.10.refs_0_ = bf16[8,96,128]{2,1,0:T(8,128)(2,1)S(1)} all-to-all(bf16[8,96,128]{2,1,0:T(8,128)(2,1)S(1)} %pack.1), channel_id=1, replica_groups=mesh['group'=4,'head'=8] {'head'}, dimensions={0} | all-to-all | bytes 393216 | tf_op jit(solution)/shard_map/all_to_all | solution.py:230
  16.1 0.0 copy-start.1
  16.1 0.0 copy-start.2
  16.1 0.1 collective-permute-start
  16.2 1.6 %collective-permute-start.1 = (bf16[8,64,128]{2,1,0:T(8,128)(2,1)S(1)}, bf16[8,64,128]{2,1,0:T(8,128)(2,1)S(1)}, u32[]{:S(2)}, u32[]{:S(2)}) collective-permute-start(bf16[8,64,128]{2,1,0:T(8,128)(2,1)S(1)} %slice.4), channel_id=1, source_target_pairs={{8,16},{16,8},{24,0},{0,24},{9,17},{17,9},{25,1},{1,25},{10,18},{1... | collective-permute-start | bytes 393224 | tf_op jit(solution)/shard_map/ppermute | solution.py:238
  17.8 0.0 collective-permute-done.refs_1_
  17.8 0.0 copy-done.1
  17.8 0.0 copy-done.2
  17.8 2.3 %attend.1 = (f32[4,88,128]{2,1,0:T(8,128)S(1)}, bf16[8,64,128]{2,1,0:T(8,128)(2,1)S(1)}) custom-call(bf16[8,96,128]{2,1,0:T(8,128)(2,1)S(1)} %all_to_all.10.refs_0_, bf16[8,64,128]{2,1,0:T(8,128)(2,1)S(1)} %collective-permute-done.refs_1_, s32[3,6,1,8]{3,2,1,0:T(1,128)S(1)} %bitcast.4, s32[3,1,8]{2,1,0:T(1,128)S(1)} %bitcast.6), custom_call_target="tpu_custom_call" | custom-call | flops 268435456 | bytes 393216 | tf_op jit(solution)/shard_map/attend/pallas_call | solution.py:197
  20.1 1.4 %collective-permute-done.1.refs_1_ = bf16[8,64,128]{2,1,0:T(8,128)(2,1)S(1)} collective-permute-done((bf16[8,64,128]{2,1,0:T(8,128)(2,1)S(1)}, bf16[8,64,128]{2,1,0:T(8,128)(2,1)S(1)}, u32[]{:S(2)}, u32[]{:S(2)}) %collective-permute-start.1) | collective-permute-done | bytes 131104 | tf_op jit(solution)/shard_map/ppermute | solution.py:238
  21.5 1.9 %attend_last.1 = bf16[8,32,128]{2,1,0:T(8,128)(2,1)S(1)} custom-call(bf16[8,64,128]{2,1,0:T(8,128)(2,1)S(1)} %get-tuple-element.7.refs_0_, bf16[8,64,128]{2,1,0:T(8,128)(2,1)S(1)} %collective-permute-done.1.refs_1_, s32[3,6,1,8]{3,2,1,0:T(1,128)S(1)} %bitcast.5, s32[3,1,8]{2,1,0:T(1,128)S(1)} %bitcast.7, f32[4,88,128]{2,1,0:T(8,128)S(1)} %get-tuple-element.8.refs_4_), custom_call_target="tpu_custom_call" | custom-call | flops 134217728 | bytes 262144 | tf_op jit(solution)/shard_map/attend_last/pallas_call | solution.py:197
  23.4 9.9 %all_to_all.11.x_ref = bf16[8,32,128]{2,1,0:T(8,128)(2,1)S(1)} all-to-all(bf16[8,32,128]{2,1,0:T(8,128)(2,1)S(1)} %attend_last.1), channel_id=1, replica_groups=mesh['group'=4,'head'=8] {'head'}, dimensions={0} | all-to-all | bytes 131072 | tf_op jit(solution)/shard_map/all_to_all | solution.py:254
  33.2 0.7 %unpack.1 = bf16[64,512]{1,0:T(8,128)(2,1)} custom-call(bf16[8,32,128]{2,1,0:T(8,128)(2,1)S(1)} %all_to_all.11.x_ref), custom_call_target="tpu_custom_call" | custom-call | tf_op jit(solution)/shard_map/unpack/pallas_call | solution.py:255
  (1 shorter events, 0.0 us)
Async XLA Ops:
  0.0 0.9 %copy-start = (bf16[64,3,512]{2,0,1:T(8,128)(2,1)S(1)}, bf16[64,3,512]{2,0,1:T(8,128)(2,1)}, u32[]{:S(2)}) copy-start(bf16[64,3,512]{2,0,1:T(8,128)(2,1)} %param.3) | copy-start | bytes 589828
  16.1 1.7 %copy-start.1 = (s32[1,3,8,6]{2,0,3,1:T(1,128)S(1)}, s32[1,3,8,6]{2,0,3,1:T(1,128)}, u32[]{:S(2)}) copy-start(s32[1,3,8,6]{2,0,3,1:T(1,128)} %param.4) | copy-start | bytes 1732
  16.1 1.7 %copy-start.2 = (s32[1,3,8]{2,0,1:T(1,128)S(1)}, s32[1,3,8]{2,0,1:T(1,128)}, u32[]{:S(2)}) copy-start(s32[1,3,8]{2,0,1:T(1,128)} %param.5) | copy-start | bytes 292
  16.1 1.7 %collective-permute-start = (bf16[8,64,128]{2,1,0:T(8,128)(2,1)S(1)}, bf16[8,64,128]{2,1,0:T(8,128)(2,1)S(1)}, u32[]{:S(2)}, u32[]{:S(2)}) collective-permute-start(bf16[8,64,128]{2,1,0:T(8,128)(2,1)S(1)} %slice.4), channel_id=1, source_target_pairs={{0,8},{8,0},{16,24},{24,16},{1,9},{9,1},{17,25},{25,17},{2,10},{10... | collective-permute-start | bytes 393224 | tf_op jit(solution)/shard_map/ppermute | solution.py:238
  16.2 5.2 %collective-permute-start.1 = (bf16[8,64,128]{2,1,0:T(8,128)(2,1)S(1)}, bf16[8,64,128]{2,1,0:T(8,128)(2,1)S(1)}, u32[]{:S(2)}, u32[]{:S(2)}) collective-permute-start(bf16[8,64,128]{2,1,0:T(8,128)(2,1)S(1)} %slice.4), channel_id=1, source_target_pairs={{8,16},{16,8},{24,0},{0,24},{9,17},{17,9},{25,1},{1,25},{10,18},{1... | collective-permute-start | bytes 393224 | tf_op jit(solution)/shard_map/ppermute | solution.py:238

commit v2 on v1

--- a/solution.py
+++ b/solution.py
@@ -79,7 +79,8 @@
     refs = list(refs)
     chunk_ref = refs.pop(0)
     sources = [refs.pop(0) for _ in kinds[first:]]
-    lists_ref, counts_ref = refs.pop(0), refs.pop(0)
+    if first or not dense:
+        lists_ref, counts_ref = refs.pop(0), refs.pop(0)
     state_ref = None if first else refs.pop(0)
     out_ref = refs.pop(0)
     query_ref = refs.pop(0) if first else chunk_ref
@@ -172,7 +173,7 @@
         pl.loop(0, blocks // per)(one_tile)
 
 
-TILE_BLOCKS = 2
+TILE_BLOCKS = 8
 
 
 def attend(chunk, kinds, sources, lists, counts, state, last, dense, dim, half, bias_for=None):
@@ -188,8 +189,11 @@
     outs = (out, jax.ShapeDtypeStruct((blocks, block, 2 * dim), jnp.bfloat16)) if first else (out,)
     vmem = pl.BlockSpec(memory_space=VMEM)
     smem = pl.BlockSpec(memory_space=SMEM)
-    args = [chunk, *sources, lists, counts]
-    specs = [vmem] * (1 + len(sources)) + [smem, smem]
+    args = [chunk, *sources]
+    specs = [vmem] * (1 + len(sources))
+    if first or not dense:
+        args += [lists, counts]
+        specs += [smem, smem]
     if not first:
         args.append(state)
         specs.append(vmem)

time: 34.1 us -> 33.1 us (0.971)
  Pallas kernels: 4.99 us -> 3.55 us
  waiting for transfers between devices: 1.37 us -> 1.77 us
    pallas_call x2, Pallas kernels: 4.16 us -> 2.72 us  [attend(): pl.pallas_call(functools.partial(attend_kernel, dim, dense, kinds, half,...]
    ppermute x2, waiting for transfers between devices: 1.37 us -> 1.77 us  [swap(): return lax.ppermute(value, 'group', pairs)]
  transfers between devices with their start and end apart: 2 -> 2, of which waited for: 1 -> 1; matrix products, arithmetic and copies ran while one was open for 0% -> 0% of each run, Pallas kernels for 7% -> 6%
where the time goes in v2:
time: 33.1 us; the launch traced here: 32.9 us
  blocking collectives  24.9 us (75%)
  Pallas kernels  3.55 us (11%)
  waiting for transfers between devices  1.77 us (5%)
  starting transfers between devices  1.66 us (5%)
  local copies, waits for them, and re-layouts  0.95 us (3%)
    all_to_all x1, blocking collectives, body(): lax.all_to_all(packed, 'head', split_axis=0, concat_axis=0, tiled=True)  15.1 us
    all_to_all x1, blocking collectives, body(): lax.all_to_all(state, 'head', split_axis=0, concat_axis=0, tiled=True)  9.85 us
    pallas_call x2, Pallas kernels, attend(): pl.pallas_call(functools.partial(attend_kernel, dim, dense, kinds, half,...  2.72 us
    ppermute x2, waiting for transfers between devices, swap(): return lax.ppermute(value, 'group', pairs)  1.77 us
    ppermute x2, starting transfers between devices, swap(): return lax.ppermute(value, 'group', pairs)  1.66 us
    unnamed x6, local copies, waits for them, and re-layouts  0.94 us
    pallas_call x1, Pallas kernels, body(): pl.pallas_call(functools.partial(unpack_kernel, dim), out_shape=jax.Shape...  0.71 us
  transfers between devices with their start and end apart: 2, of which 1 were waited for; matrix products, arithmetic and copies ran while one was open for 0% of the time, Pallas kernels for 6%

profile of v2, /device:TPU:0, one launch (start us, length us, event | category | flops | bytes accessed | tf_op | source)
XLA Modules:
  0.0 32.9 jit_solution(1006451327431247623)
XLA Ops:
  0.0 0.0 copy-start
  0.0 0.9 %copy-done = bf16[64,3,512]{2,0,1:T(8,128)(2,1)S(1)} copy-done((bf16[64,3,512]{2,0,1:T(8,128)(2,1)S(1)}, bf16[64,3,512]{2,0,1:T(8,128)(2,1)}, u32[]{:S(2)}) %copy-start) | copy-done | bytes 196632
  0.9 0.1 pack.1
  1.1 15.1 %all_to_all.10.refs_0_ = bf16[8,96,128]{2,1,0:T(8,128)(2,1)S(1)} all-to-all(bf16[8,96,128]{2,1,0:T(8,128)(2,1)S(1)} %pack.1), channel_id=1, replica_groups=mesh['group'=4,'head'=8] {'head'}, dimensions={0} | all-to-all | bytes 393216 | tf_op jit(solution)/shard_map/all_to_all | solution.py:234
  16.1 0.0 copy-start.1
  16.1 0.0 copy-start.2
  16.1 0.1 collective-permute-start
  16.2 1.6 %collective-permute-start.1 = (bf16[8,64,128]{2,1,0:T(8,128)(2,1)S(1)}, bf16[8,64,128]{2,1,0:T(8,128)(2,1)S(1)}, u32[]{:S(2)}, u32[]{:S(2)}) collective-permute-start(bf16[8,64,128]{2,1,0:T(8,128)(2,1)S(1)} %slice.4), channel_id=1, source_target_pairs={{8,16},{16,8},{24,0},{0,24},{9,17},{17,9},{25,1},{1,25},{10,18},{1... | collective-permute-start | bytes 393224 | tf_op jit(solution)/shard_map/ppermute | solution.py:242
  17.8 0.0 collective-permute-done.refs_1_
  17.8 0.0 copy-done.1
  17.8 0.0 copy-done.2
  17.8 1.9 %attend.1 = (f32[1,88,512]{2,1,0:T(8,128)S(1)}, bf16[8,64,128]{2,1,0:T(8,128)(2,1)S(1)}) custom-call(bf16[8,96,128]{2,1,0:T(8,128)(2,1)S(1)} %all_to_all.10.refs_0_, bf16[8,64,128]{2,1,0:T(8,128)(2,1)S(1)} %collective-permute-done.refs_1_, s32[3,6,1,8]{3,2,1,0:T(1,128)S(1)} %bitcast.4, s32[3,1,8]{2,1,0:T(1,128)S(1)} %bitcast.5), custom_call_target="tpu_custom_call" | custom-call | flops 268435456 | bytes 393216 | tf_op jit(solution)/shard_map/attend/pallas_call | solution.py:201
  19.7 1.8 %collective-permute-done.1.refs_1_ = bf16[8,64,128]{2,1,0:T(8,128)(2,1)S(1)} collective-permute-done((bf16[8,64,128]{2,1,0:T(8,128)(2,1)S(1)}, bf16[8,64,128]{2,1,0:T(8,128)(2,1)S(1)}, u32[]{:S(2)}, u32[]{:S(2)}) %collective-permute-start.1) | collective-permute-done | bytes 131104 | tf_op jit(solution)/shard_map/ppermute | solution.py:242
  21.5 0.8 %attend_last.1 = bf16[8,32,128]{2,1,0:T(8,128)(2,1)S(1)} custom-call(bf16[8,64,128]{2,1,0:T(8,128)(2,1)S(1)} %get-tuple-element.7.refs_0_, bf16[8,64,128]{2,1,0:T(8,128)(2,1)S(1)} %collective-permute-done.1.refs_1_, f32[1,88,512]{2,1,0:T(8,128)S(1)} %get-tuple-element.8.refs_2_), custom_call_target="tpu_custom_call" | custom-call | flops 134217728 | bytes 262144 | tf_op jit(solution)/shard_map/attend_last/pallas_call | solution.py:201
  22.3 9.9 %all_to_all.11.x_ref = bf16[8,32,128]{2,1,0:T(8,128)(2,1)S(1)} all-to-all(bf16[8,32,128]{2,1,0:T(8,128)(2,1)S(1)} %attend_last.1), channel_id=1, replica_groups=mesh['group'=4,'head'=8] {'head'}, dimensions={0} | all-to-all | bytes 131072 | tf_op jit(solution)/shard_map/all_to_all | solution.py:258
  32.2 0.7 %unpack.1 = bf16[64,512]{1,0:T(8,128)(2,1)} custom-call(bf16[8,32,128]{2,1,0:T(8,128)(2,1)S(1)} %all_to_all.11.x_ref), custom_call_target="tpu_custom_call" | custom-call | tf_op jit(solution)/shard_map/unpack/pallas_call | solution.py:259
  (1 shorter events, 0.0 us)
Async XLA Ops:
  0.0 0.9 %copy-start = (bf16[64,3,512]{2,0,1:T(8,128)(2,1)S(1)}, bf16[64,3,512]{2,0,1:T(8,128)(2,1)}, u32[]{:S(2)}) copy-start(bf16[64,3,512]{2,0,1:T(8,128)(2,1)} %param.3) | copy-start | bytes 589828
  16.1 1.7 %copy-start.1 = (s32[1,3,8,6]{2,0,3,1:T(1,128)S(1)}, s32[1,3,8,6]{2,0,3,1:T(1,128)}, u32[]{:S(2)}) copy-start(s32[1,3,8,6]{2,0,3,1:T(1,128)} %param.4) | copy-start | bytes 1732
  16.1 1.7 %copy-start.2 = (s32[1,3,8]{2,0,1:T(1,128)S(1)}, s32[1,3,8]{2,0,1:T(1,128)}, u32[]{:S(2)}) copy-start(s32[1,3,8]{2,0,1:T(1,128)} %param.5) | copy-start | bytes 292
  16.1 1.7 %collective-permute-start = (bf16[8,64,128]{2,1,0:T(8,128)(2,1)S(1)}, bf16[8,64,128]{2,1,0:T(8,128)(2,1)S(1)}, u32[]{:S(2)}, u32[]{:S(2)}) collective-permute-start(bf16[8,64,128]{2,1,0:T(8,128)(2,1)S(1)} %slice.4), channel_id=1, source_target_pairs={{0,8},{8,0},{16,24},{24,16},{1,9},{9,1},{17,25},{25,17},{2,10},{10... | collective-permute-start | bytes 393224 | tf_op jit(solution)/shard_map/ppermute | solution.py:242
  16.2 5.2 %collective-permute-start.1 = (bf16[8,64,128]{2,1,0:T(8,128)(2,1)S(1)}, bf16[8,64,128]{2,1,0:T(8,128)(2,1)S(1)}, u32[]{:S(2)}, u32[]{:S(2)}) collective-permute-start(bf16[8,64,128]{2,1,0:T(8,128)(2,1)S(1)} %slice.4), channel_id=1, source_target_pairs={{8,16},{16,8},{24,0},{0,24},{9,17},{17,9},{25,1},{1,25},{10,18},{1... | collective-permute-start | bytes 393224 | tf_op jit(solution)/shard_map/ppermute | solution.py:242
